TPU v7x, 32 devices: a whole 2x2x4 slice. The times are simulated.
32 devices in a mesh: row: 4 (over y, x), col: 8 (over z, core).
Axes of the slice: x: 2, y: 2, z: 4, core: 2. Of those that a mesh axis runs over, the one named last changes fastest.
Arguments:
- node_features: bfloat16 [2048, 128, 512], P(('row', 'col')), may hold values from -6 to 6
- node_counts: int32 [2048], P(('row', 'col')), may hold values from 16 to 128, as said below
- edge_list: int32 [2048, 2, 256], P(('row', 'col')), may hold values from 0 to 128, as said below
- readout_ids: int32 [2048], P(('row', 'col')), may hold values from 0 to 255
- live_graphs: int32 [32], P(('row', 'col')), may hold values from 1 to 64, as said below
- self_weight: float32 [1], replicated, may hold values from 0.5 to 1.5
- w_first: bfloat16 [512, 512], replicated, may hold values from -0.25 to 0.25
- b_first: float32 [512], replicated, may hold values from -3 to 3
- w_second: bfloat16 [512, 512], replicated, may hold values from -0.25 to 0.25
- b_second: float32 [512], replicated, may hold values from -3 to 3
- w_third: bfloat16 [512, 512], replicated, may hold values from -0.25 to 0.25
- b_third: float32 [512], replicated, may hold values from -3 to 3
Outputs:
- node_out: bfloat16 [1024, 128, 512], P(('row', 'col'))
- readout: float32 [256, 512], P(('row', 'col'))
Inputs may be any that keep to these rules, and one draw needn't show every extreme that they name: `live_graphs`: the entries sum to 1024, and at least one equals 64. `node_counts`: node slots 0 to count - 1 of a graph are live; the rest of its block is padding. `edge_list`: each edge slot holds two node indices below its graph's node count, or 128 in both rows for an unused slot.
All inputs are finite; a program needn't handle non-finite values.
Results may differ from a plain program's by a relative error of at most 0.0058.
Values may be sent and summed in bfloat16 or wider, within the bound.
A program may use at most 128 MiB of HBM per device.

v0:
```python
import jax
import jax.numpy as jnp
from jax import lax
from jax.sharding import PartitionSpec as P

G_DEV = 32
READ_DEV = 8


def blend_nodes(features, edge_slots, self_weight):
    node_index = lax.broadcasted_iota(jnp.int32, (1, 1, features.shape[1]), 2)
    sources = (edge_slots[:, 0, :, None] == node_index).astype(jnp.bfloat16)
    targets = (edge_slots[:, 1, :, None] == node_index).astype(jnp.bfloat16)
    adjacency = jnp.einsum(
        "gek,gel->gkl", targets, sources, preferred_element_type=jnp.float32
    ).astype(jnp.bfloat16)
    neighbour = jnp.einsum("gkl,glh->gkh", adjacency, features, preferred_element_type=jnp.float32)
    return (self_weight[0] * features.astype(jnp.float32) + neighbour).astype(jnp.bfloat16)


def perceptron(blended, weights):
    w_first, b_first, w_second, b_second, w_third, b_third = weights
    flat_rows = blended.reshape(-1, blended.shape[-1])
    hidden_one = jax.nn.relu(
        jnp.dot(flat_rows, w_first, preferred_element_type=jnp.float32) + b_first
    ).astype(jnp.bfloat16)
    hidden_two = jax.nn.relu(
        jnp.dot(hidden_one, w_second, preferred_element_type=jnp.float32) + b_second
    ).astype(jnp.bfloat16)
    result = jnp.dot(hidden_two, w_third, preferred_element_type=jnp.float32) + b_third
    return result.reshape(blended.shape)


def arrival_index(slot_tags):
    wanted = lax.broadcasted_iota(jnp.int32, (G_DEV, slot_tags.shape[0]), 0)
    places = lax.broadcasted_iota(jnp.int32, (G_DEV, slot_tags.shape[0]), 1)
    return jnp.sum(jnp.where(slot_tags[None, :] == wanted, places, 0), axis=1)


def readout_terms(graph_ids, pooled, row_count):
    id_keys = lax.broadcasted_iota(jnp.int32, (row_count, graph_ids.shape[0]), 0)
    members = (id_keys == graph_ids[None, :]).astype(jnp.float32)
    return jnp.dot(
        members, pooled, precision=lax.Precision.HIGHEST, preferred_element_type=jnp.float32
    )


def body(
    node_features,
    node_counts,
    edge_list,
    readout_ids,
    live_graphs,
    self_weight,
    w_first,
    b_first,
    w_second,
    b_second,
    w_third,
    b_third,
):
    weights = (w_first, b_first, w_second, b_second, w_third, b_third)
    devices = lax.axis_size(("row", "col"))
    capacity = node_features.shape[0]
    bucket = (capacity + devices - 1) // devices
    own_count = live_graphs[0]
    every_count = lax.all_gather(live_graphs, ("row", "col"), axis=0, tiled=True)
    position = lax.broadcasted_iota(jnp.int32, (devices,), 0)
    offset = jnp.sum(jnp.where(position < lax.axis_index(("row", "col")), every_count, 0))
    targets = lax.broadcasted_iota(jnp.int32, (devices * bucket,), 0)
    dest_device = targets // bucket
    within = (dest_device - offset) % devices + targets % bucket * devices
    sending_ok = within < own_count
    slot_tags = jnp.where(sending_ok, (offset + within) // devices, G_DEV)
    picked = jnp.minimum(within, capacity - 1)
    node_index = lax.broadcasted_iota(jnp.int32, (1, node_features.shape[1]), 1)
    blended = blend_nodes(node_features, edge_list, self_weight)
    live_nodes = node_index < node_counts[:, None]
    results = jnp.where(live_nodes[:, :, None], perceptron(blended, weights), 0.0).astype(
        jnp.bfloat16
    )
    pooled = jnp.sum(results.astype(jnp.float32), axis=1) / node_counts[:, None].astype(jnp.float32)
    slot_live = lax.broadcasted_iota(jnp.int32, (capacity,), 0) < own_count
    graph_ids = jnp.where(slot_live, readout_ids, -1)
    arrived, arrived_tags = (
        lax.all_to_all(results[picked], ("row", "col"), split_axis=0, concat_axis=0, tiled=True),
        lax.all_to_all(slot_tags, ("row", "col"), split_axis=0, concat_axis=0, tiled=True),
    )
    node_out = arrived[arrival_index(arrived_tags)]
    totals = lax.psum(readout_terms(graph_ids, pooled, READ_DEV * devices), ("row", "col"))
    readout = lax.dynamic_slice_in_dim(
        totals, lax.axis_index(("row", "col")) * READ_DEV, READ_DEV, 0
    )
    return (node_out, readout)


def solution(mesh):
    in_specs = (
        P(("row", "col"), None, None),
        P(("row", "col")),
        P(("row", "col"), None, None),
        P(("row", "col")),
        P(("row", "col")),
        P(),
        P(),
        P(),
        P(),
        P(),
        P(),
        P(),
    )
    out_specs = (P(("row", "col"), None, None), P(("row", "col"), None))
    return jax.shard_map(body, mesh=mesh, in_specs=in_specs, out_specs=out_specs, check_vma=False)
```

profile of v0, /device:TPU:0, one launch (start us, length us, event | category | flops | bytes accessed | tf_op | source)
XLA Modules:
  0.0 323.4 jit_solution(11251081128402884339)
XLA Ops:
  7.9 0.1 dynamic-update-slice
  8.0 41.9 %all-reduce = s32[32]{0:T(128)S(1)} all-reduce(s32[32]{0:T(128)S(1)} %dynamic-update-slice), channel_id=1, replica_groups=mesh['row'=4,'col'=8] {'row','col'}, use_global_device_ids=true, to_apply=%add | all-reduce | flops 32 | bytes 256
  50.0 0.6 fusion.15
  50.6 1.4 compare_select_fusion.2
  52.0 4.4 %all-to-all-start.1 = ((s32[32,2,1]{1,2,0:T(1,128)}), s32[32,2,1]{1,2,0:T(1,128)S(1)}, u32[]{:S(2)}, u32[]{:S(2)}) async-start(s32[32,2,1]{1,2,0:T(1,128)} %compare_select_fusion.2), calls=%async_computation.1 | async-start | bytes 32768 | tf_op jit(solution)/shard_map/all_to_all | solution.py:87
  56.4 0.7 fusion.17
  57.1 1.1 fusion.20
  58.8 0.7 iota_compare_fusion.14
  59.6 12.6 %add_convert_fusion = bf16[64,128,512]{2,1,0:T(8,128)(2,1)} fusion(bf16[64,128,512]{2,1,0:T(8,128)(2,1)} %param.12, f32[]{:T(128)} %bitcast.24, s32[64,256]{1,0:T(8,128)S(1)} %get-tuple-element.6, s32[64,256]{1,0:T(8,128)S(1)} %get-tuple-element.7), kind=kOutput, calls=%fused_computation.6 | convolution fusion | flops 1632632832 | bytes 16908292 | tf_op jit(solution)/shard_map/gkl,glh->gkh/dot_general | solution.py:17
  72.2 10.2 %maximum_convert_fusion.1 = bf16[8192,512]{1,0:T(8,128)(2,1)} fusion(bf16[8192,512]{1,0:T(8,128)(2,1)} %bitcast.25, bf16[512,512]{1,0:T(8,128)(2,1)S(1)} %copy-done, f32[512]{0:T(512)S(1)} %copy-done.4), kind=kOutput, calls=%fused_computation.5 | convolution fusion | flops 4307550208 | bytes 17303552 | tf_op jit(solution)/shard_map/dot_general | solution.py:25
  82.5 13.3 %convolution_add_fusion = bf16[8192,512]{1,0:T(8,128)(2,1)} fusion(bf16[512,512]{1,0:T(8,128)(2,1)S(1)} %copy-done.2, f32[512]{0:T(512)S(1)} %copy-done.5, bf16[8192,512]{1,0:T(8,128)(2,1)} %maximum_convert_fusion.1, bf16[512,512]{1,0:T(8,128)(2,1)S(1)} %copy-done.3, f32[512]{0:T(512)S(1)} %copy-done.6), kind=kOutput, calls=%fused_computation.7 | convolution fusion | flops 8610906112 | bytes 17829888 | tf_op jit(solution)/shard_map/dot_general | solution.py:30
  95.7 8.3 %convert_reduce_fusion = (f32[64,512]{1,0:T(8,128)S(1)}, bf16[64,128,512]{2,1,0:T(8,128)(2,1)}) fusion(pred[64,128]{1,0:T(8,128)(4,1)S(1)} %iota_compare_fusion.14, bf16[8192,512]{1,0:T(8,128)(2,1)} %convolution_add_fusion), kind=kLoop, calls=%fused_computation.2 | loop fusion | flops 12550144 | bytes 16916480 | tf_op jit(solution)/shard_map/reduce_sum | solution.py:82
  104.1 8.9 %gather_fusion = bf16[64,128,512]{2,1,0:T(8,128)(2,1)} fusion(bf16[64,128,512]{2,1,0:T(8,128)(2,1)} %get-tuple-element.3, s32[1024]{0:T(1024)S(1)} %pad_clamp_fusion.1), kind=kCustom, calls=%fused_computation | custom fusion | bytes 16777472 | tf_op jit(solution)/shard_map/gather | solution.py:86
  113.0 6.0 %all-to-all-start = ((bf16[64,128,512]{2,1,0:T(8,128)(2,1)}), bf16[64,128,512]{2,1,0:T(8,128)(2,1)}, u32[]{:S(2)}, u32[]{:S(2)}) async-start(bf16[64,128,512]{2,1,0:T(8,128)(2,1)} %gather_fusion), calls=%async_computation | async-start | bytes 16777216 | tf_op jit(solution)/shard_map/all_to_all | solution.py:86
  119.0 0.0 all-reduce.3.cloned.1.call-start
  119.0 1.2 fusion.4
  120.3 0.5 broadcast.399
  120.8 0.7 reduce.3
  121.5 0.1 eq.59
  121.6 0.1 select_reduce_fusion
  121.8 173.9 %all-reduce.3.cloned.1.call-done = f32[256,512]{1,0:T(8,128)} async-done(((f32[256,512]{1,0:T(8,128)}), f32[256,512]{1,0:T(8,128)}) %all-reduce.3.cloned.1.call-update) | async-done | bytes 524304 | tf_op jit(solution)/shard_map/psum | solution.py:90
  295.6 1.3 constant_dynamic-slice_fusion
  297.0 13.4 %all-to-all-done = bf16[64,128,512]{2,1,0:T(8,128)(2,1)} async-done(((bf16[64,128,512]{2,1,0:T(8,128)(2,1)}), bf16[64,128,512]{2,1,0:T(8,128)(2,1)}, u32[]{:S(2)}, u32[]{:S(2)}) %all-to-all-start) | async-done | bytes 8388640 | tf_op jit(solution)/shard_map/all_to_all | solution.py:86
  310.4 6.2 %gather_fusion.1 = bf16[32,128,512]{2,1,0:T(8,128)(2,1)} fusion(bf16[64,128,512]{2,1,0:T(8,128)(2,1)} %all-to-all-done, s32[1024]{0:T(1024)S(1)} %pad_clamp_fusion), kind=kCustom, calls=%fused_computation.1 | custom fusion | bytes 8388736 | tf_op jit(solution)/shard_map/gather | solution.py:89
  (25 shorter events, 0.1 us)
Async XLA Ops:
  7.2 65.0 %copy-start = (bf16[512,512]{1,0:T(8,128)(2,1)S(1)}, bf16[512,512]{1,0:T(8,128)(2,1)}, u32[]{:S(2)}) copy-start(bf16[512,512]{1,0:T(8,128)(2,1)} %param.18) | copy-start | bytes 1572868
  52.0 61.0 %all-to-all-start.1 = ((s32[32,2,1]{1,2,0:T(1,128)}), s32[32,2,1]{1,2,0:T(1,128)S(1)}, u32[]{:S(2)}, u32[]{:S(2)}) async-start(s32[32,2,1]{1,2,0:T(1,128)} %compare_select_fusion.2), calls=%async_computation.1 | async-start | bytes 32768 | tf_op jit(solution)/shard_map/all_to_all | solution.py:87
  59.6 12.6 %copy-start.4 = (f32[512]{0:T(512)S(1)}, f32[512]{0:T(512)}, u32[]{:S(2)}) copy-start(f32[512]{0:T(512)} %param.19) | copy-start | bytes 6148
  72.2 10.3 %copy-start.2 = (bf16[512,512]{1,0:T(8,128)(2,1)S(1)}, bf16[512,512]{1,0:T(8,128)(2,1)}, u32[]{:S(2)}) copy-start(bf16[512,512]{1,0:T(8,128)(2,1)} %param.22) | copy-start | bytes 1572868
  72.2 10.3 %copy-start.3 = (bf16[512,512]{1,0:T(8,128)(2,1)S(1)}, bf16[512,512]{1,0:T(8,128)(2,1)}, u32[]{:S(2)}) copy-start(bf16[512,512]{1,0:T(8,128)(2,1)} %param.20) | copy-start | bytes 1572868
  72.2 10.3 %copy-start.5 = (f32[512]{0:T(512)S(1)}, f32[512]{0:T(512)}, u32[]{:S(2)}) copy-start(f32[512]{0:T(512)} %param.23) | copy-start | bytes 6148
  72.2 10.3 %copy-start.6 = (f32[512]{0:T(512)S(1)}, f32[512]{0:T(512)}, u32[]{:S(2)}) copy-start(f32[512]{0:T(512)} %param.21) | copy-start | bytes 6148
  113.0 6.0 %copy-start.1 = (s32[64]{0:T(128)S(1)}, s32[64]{0:T(128)}, u32[]{:S(2)}) copy-start(s32[64]{0:T(128)} %param.13) | copy-start | bytes 772
  113.0 6.1 %copy-start.7 = (s32[64]{0:T(128)S(1)}, s32[64]{0:T(128)}, u32[]{:S(2)}) copy-start(s32[64]{0:T(128)} %param.15) | copy-start | bytes 772
  113.0 197.4 %all-to-all-start = ((bf16[64,128,512]{2,1,0:T(8,128)(2,1)}), bf16[64,128,512]{2,1,0:T(8,128)(2,1)}, u32[]{:S(2)}, u32[]{:S(2)}) async-start(bf16[64,128,512]{2,1,0:T(8,128)(2,1)} %gather_fusion), calls=%async_computation | async-start | bytes 16777216 | tf_op jit(solution)/shard_map/all_to_all | solution.py:86
  119.0 176.7 %all-reduce.3.cloned.1.call-start = ((), (), s32[]{:S(2)}) async-start(), calls=%async_computation.2 | async-start | bytes 1048576 | tf_op jit(solution)/shard_map/psum | solution.py:90
Sparse Core Ops, SparseCore 0:
  125.6 169.9 all-reduce.2
where the time goes:
time: 324 us; the launch traced here: 323 us
  waiting for transfers between devices  187 us (58%)
  blocking collectives  41.9 us (13%)
  matrix products  37.3 us (12%)
  local copies, waits for them, and re-layouts  18.3 us (6%)
  between operations  15.6 us (5%)
  other arithmetic  12.6 us (4%)
  starting transfers between devices  10.4 us (3%)
    psum x1, waiting for transfers between devices, body(): lax.psum(readout_terms(graph_ids, pooled, READ_DEV * devices), ('row', 'c...  174 us
    unnamed x1, blocking collectives  41.9 us
    all_to_all x1, waiting for transfers between devices, body(): lax.all_to_all(results[picked], ('row', 'col'), split_axis=0, concat_axis...  13.4 us
    dot_general x1, matrix products, perceptron(): jnp.dot(hidden_two, w_third, preferred_element_type=jnp.float32) + b_third  13.3 us
    dot_general x1, matrix products, blend_nodes(): jnp.einsum('gkl,glh->gkh', adjacency, features, preferred_element_type=jn...  12.6 us
    dot_general x1, matrix products, perceptron(): jnp.dot(flat_rows, w_first, preferred_element_type=jnp.float32) + b_first  10.2 us
    gather x1, local copies, waits for them, and re-layouts, body(): results[picked]  8.91 us
    reduce_sum x1, other arithmetic, body(): jnp.sum(results.astype(jnp.float32), axis=1)  8.33 us
  transfers between devices with their start and end apart: 3, of which 2 were waited for; matrix products, arithmetic and copies ran while one was open for 18% of the time, Pallas kernels for 0%

commit v1 on v0

--- a/solution.py
+++ b/solution.py
@@ -87,7 +87,9 @@
         lax.all_to_all(slot_tags, ("row", "col"), split_axis=0, concat_axis=0, tiled=True),
     )
     node_out = arrived[arrival_index(arrived_tags)]
-    totals = lax.psum(readout_terms(graph_ids, pooled, READ_DEV * devices), ("row", "col"))
+    x = readout_terms(graph_ids, pooled, READ_DEV * devices)
+    parts = lax.all_gather(x, ("row", "col"))
+    totals = jnp.sum(parts, axis=0)
     readout = lax.dynamic_slice_in_dim(
         totals, lax.axis_index(("row", "col")) * READ_DEV, READ_DEV, 0
     )

time: 324 us -> 374 us (1.15)
  waiting for transfers between devices: 187 us -> 228 us
  other arithmetic: 12.6 us -> 20.9 us
    all_to_all x1, waiting for transfers between devices: 13.4 us -> 228 us  [body(): lax.all_to_all(results[picked], ('row', 'col'), split_axis=0, concat_axis...]
    psum x1 -> x0, waiting for transfers between devices: 174 us -> none  [body(): lax.psum(readout_terms(graph_ids, pooled, READ_DEV * devices), ('row', 'c...]
    reduce_sum x0 -> x1, other arithmetic: none -> 7.81 us  [body(): totals = jnp.sum(parts, axis=0)]
  transfers between devices with their start and end apart: 3 -> 3, of which waited for: 2 -> 1; matrix products, arithmetic and copies ran while one was open for 18% -> 5% of each run, Pallas kernels for 0% -> 0%
where the time goes in v1:
time: 374 us; the launch traced here: 373 us
  waiting for transfers between devices  228 us (61%)
  blocking collectives  43.6 us (12%)
  matrix products  37.3 us (10%)
  other arithmetic  20.9 us (6%)
  local copies, waits for them, and re-layouts  17.7 us (5%)
  between operations  15.5 us (4%)
  starting transfers between devices  10.2 us (3%)
    all_to_all x1, waiting for transfers between devices, body(): lax.all_to_all(results[picked], ('row', 'col'), split_axis=0, concat_axis...  228 us
    unnamed x1, blocking collectives  43.6 us
    dot_general x1, matrix products, perceptron(): jnp.dot(hidden_two, w_third, preferred_element_type=jnp.float32) + b_third  13.3 us
    dot_general x1, matrix products, blend_nodes(): jnp.einsum('gkl,glh->gkh', adjacency, features, preferred_element_type=jn...  12.6 us
    dot_general x1, matrix products, perceptron(): jnp.dot(flat_rows, w_first, preferred_element_type=jnp.float32) + b_first  10.2 us
    gather x1, local copies, waits for them, and re-layouts, body(): results[picked]  9.01 us
    reduce_sum x1, other arithmetic, body(): jnp.sum(results.astype(jnp.float32), axis=1)  8.32 us
    reduce_sum x1, other arithmetic, body(): totals = jnp.sum(parts, axis=0)  7.81 us
  transfers between devices with their start and end apart: 3, of which 1 were waited for; matrix products, arithmetic and copies ran while one was open for 5% of the time, Pallas kernels for 0%

profile of v1, /device:TPU:0, one launch (start us, length us, event | category | flops | bytes accessed | tf_op | source)
XLA Modules:
  0.0 373.4 jit_solution(9964921495333553476)
XLA Ops:
  7.2 0.8 iota_compare_fusion.14
  8.0 0.7 convert_element_type.35
  9.3 1.1 fusion.20
  11.1 12.6 %add_convert_fusion = bf16[64,128,512]{2,1,0:T(8,128)(2,1)} fusion(bf16[64,128,512]{2,1,0:T(8,128)(2,1)} %param.12, f32[]{:T(128)} %bitcast.25, s32[64,256]{1,0:T(8,128)S(1)} %get-tuple-element.6, s32[64,256]{1,0:T(8,128)S(1)} %get-tuple-element.7), kind=kOutput, calls=%fused_computation.6 | convolution fusion | flops 1632632832 | bytes 16908292 | tf_op jit(solution)/shard_map/gkl,glh->gkh/dot_general | solution.py:17
  23.7 10.2 %maximum_convert_fusion.1 = bf16[8192,512]{1,0:T(8,128)(2,1)} fusion(bf16[8192,512]{1,0:T(8,128)(2,1)} %bitcast.27, bf16[512,512]{1,0:T(8,128)(2,1)S(1)} %copy-done, f32[512]{0:T(512)S(1)} %copy-done.4), kind=kOutput, calls=%fused_computation.5 | convolution fusion | flops 4307550208 | bytes 17303552 | tf_op jit(solution)/shard_map/dot_general | solution.py:25
  34.0 13.3 %convolution_add_fusion = bf16[8192,512]{1,0:T(8,128)(2,1)} fusion(bf16[512,512]{1,0:T(8,128)(2,1)S(1)} %copy-done.2, f32[512]{0:T(512)S(1)} %copy-done.5, bf16[8192,512]{1,0:T(8,128)(2,1)} %maximum_convert_fusion.1, bf16[512,512]{1,0:T(8,128)(2,1)S(1)} %copy-done.3, f32[512]{0:T(512)S(1)} %copy-done.6), kind=kOutput, calls=%fused_computation.7 | convolution fusion | flops 8610906112 | bytes 17829888 | tf_op jit(solution)/shard_map/dot_general | solution.py:30
  47.3 8.3 %convert_reduce_fusion = (f32[64,512]{1,0:T(8,128)S(1)}, bf16[64,128,512]{2,1,0:T(8,128)(2,1)}) fusion(pred[64,128]{1,0:T(8,128)(4,1)S(1)} %iota_compare_fusion.14, bf16[8192,512]{1,0:T(8,128)(2,1)} %convolution_add_fusion), kind=kLoop, calls=%fused_computation.2 | loop fusion | flops 12550144 | bytes 16916480 | tf_op jit(solution)/shard_map/reduce_sum | solution.py:82
  55.6 1.3 fusion.4
  56.9 0.1 dynamic-update-slice
  57.0 43.6 %all-reduce = s32[32]{0:T(128)S(1)} all-reduce(s32[32]{0:T(128)S(1)} %dynamic-update-slice), channel_id=1, replica_groups=mesh['row'=4,'col'=8] {'row','col'}, use_global_device_ids=true, to_apply=%add | all-reduce | flops 32 | bytes 256
  100.6 0.6 fusion.15
  101.3 1.3 compare_select_fusion.2
  102.6 4.5 %all-to-all-start.1 = ((s32[32,2,1]{1,2,0:T(1,128)}), s32[32,2,1]{1,2,0:T(1,128)S(1)}, u32[]{:S(2)}, u32[]{:S(2)}) async-start(s32[32,2,1]{1,2,0:T(1,128)} %compare_select_fusion.2), calls=%async_computation.1 | async-start | bytes 32768 | tf_op jit(solution)/shard_map/all_to_all | solution.py:87
  107.1 0.6 fusion.17
  107.7 9.0 %gather_fusion = bf16[64,128,512]{2,1,0:T(8,128)(2,1)} fusion(bf16[64,128,512]{2,1,0:T(8,128)(2,1)} %get-tuple-element.3, s32[1024]{0:T(1024)S(1)} %pad_clamp_fusion.1), kind=kCustom, calls=%fused_computation | custom fusion | bytes 16777472 | tf_op jit(solution)/shard_map/gather | solution.py:86
  116.7 5.7 %all-to-all-start = ((bf16[64,128,512]{2,1,0:T(8,128)(2,1)}), bf16[64,128,512]{2,1,0:T(8,128)(2,1)}, u32[]{:S(2)}, u32[]{:S(2)}) async-start(bf16[64,128,512]{2,1,0:T(8,128)(2,1)} %gather_fusion), calls=%async_computation | async-start | bytes 16777216 | tf_op jit(solution)/shard_map/all_to_all | solution.py:86
  122.4 0.5 broadcast.399
  122.9 0.7 reduce.3
  123.6 0.1 eq.59
  123.7 0.1 select_reduce_fusion
  123.9 228.0 %all-to-all-done = bf16[64,128,512]{2,1,0:T(8,128)(2,1)} async-done(((bf16[64,128,512]{2,1,0:T(8,128)(2,1)}), bf16[64,128,512]{2,1,0:T(8,128)(2,1)}, u32[]{:S(2)}, u32[]{:S(2)}) %all-to-all-start) | async-done | bytes 8388640 | tf_op jit(solution)/shard_map/all_to_all | solution.py:86
  351.9 6.2 %gather_fusion.1 = bf16[32,128,512]{2,1,0:T(8,128)(2,1)} fusion(bf16[64,128,512]{2,1,0:T(8,128)(2,1)} %all-to-all-done, s32[1024]{0:T(1024)S(1)} %pad_clamp_fusion), kind=kCustom, calls=%fused_computation.1 | custom fusion | bytes 8388736 | tf_op jit(solution)/shard_map/gather | solution.py:89
  358.1 7.8 %reduce_sum.42 = f32[256,512]{1,0:T(8,128)S(1)} reduce(f32[32,256,512]{2,1,0:T(8,128)} %bitcast.26, f32[]{:T(128)} %constant.74.clone.1), dimensions={0}, to_apply=%region_3.4 | reduce | flops 4063232 | bytes 17301508 | tf_op jit(solution)/shard_map/reduce_sum | solution.py:92
  365.9 0.6 constant_dynamic-slice_fusion
  (26 shorter events, 0.1 us)
Async XLA Ops:
  7.2 16.5 %copy-start = (bf16[512,512]{1,0:T(8,128)(2,1)S(1)}, bf16[512,512]{1,0:T(8,128)(2,1)}, u32[]{:S(2)}) copy-start(bf16[512,512]{1,0:T(8,128)(2,1)} %param.18) | copy-start | bytes 1572868
  7.2 350.9 %all-gather.3.cloned.1.call-start = ((), (), s32[]{:S(2)}) async-start(), calls=%async_computation.2 | async-start | bytes 17301504 | tf_op jit(solution)/shard_map/all_gather | solution.py:91
  11.1 12.6 %copy-start.4 = (f32[512]{0:T(512)S(1)}, f32[512]{0:T(512)}, u32[]{:S(2)}) copy-start(f32[512]{0:T(512)} %param.19) | copy-start | bytes 6148
  23.7 10.3 %copy-start.2 = (bf16[512,512]{1,0:T(8,128)(2,1)S(1)}, bf16[512,512]{1,0:T(8,128)(2,1)}, u32[]{:S(2)}) copy-start(bf16[512,512]{1,0:T(8,128)(2,1)} %param.22) | copy-start | bytes 1572868
  23.7 10.3 %copy-start.3 = (bf16[512,512]{1,0:T(8,128)(2,1)S(1)}, bf16[512,512]{1,0:T(8,128)(2,1)}, u32[]{:S(2)}) copy-start(bf16[512,512]{1,0:T(8,128)(2,1)} %param.20) | copy-start | bytes 1572868
  23.7 10.3 %copy-start.5 = (f32[512]{0:T(512)S(1)}, f32[512]{0:T(512)}, u32[]{:S(2)}) copy-start(f32[512]{0:T(512)} %param.23) | copy-start | bytes 6148
  23.7 10.3 %copy-start.6 = (f32[512]{0:T(512)S(1)}, f32[512]{0:T(512)}, u32[]{:S(2)}) copy-start(f32[512]{0:T(512)} %param.21) | copy-start | bytes 6148
  47.3 8.3 %copy-start.7 = (s32[64]{0:T(128)S(1)}, s32[64]{0:T(128)}, u32[]{:S(2)}) copy-start(s32[64]{0:T(128)} %param.15) | copy-start | bytes 772
  102.6 14.1 %all-to-all-start.1 = ((s32[32,2,1]{1,2,0:T(1,128)}), s32[32,2,1]{1,2,0:T(1,128)S(1)}, u32[]{:S(2)}, u32[]{:S(2)}) async-start(s32[32,2,1]{1,2,0:T(1,128)} %compare_select_fusion.2), calls=%async_computation.1 | async-start | bytes 32768 | tf_op jit(solution)/shard_map/all_to_all | solution.py:87
  116.7 235.2 %all-to-all-start = ((bf16[64,128,512]{2,1,0:T(8,128)(2,1)}), bf16[64,128,512]{2,1,0:T(8,128)(2,1)}, u32[]{:S(2)}, u32[]{:S(2)}) async-start(bf16[64,128,512]{2,1,0:T(8,128)(2,1)} %gather_fusion), calls=%async_computation | async-start | bytes 16777216 | tf_op jit(solution)/shard_map/all_to_all | solution.py:86
  358.1 8.4 %copy-start.1 = (bf16[512,512]{1,0:T(8,128)(2,1)S(1)}, bf16[512,512]{1,0:T(8,128)(2,1)}, u32[]{:S(2)}) copy-start(bf16[512,512]{1,0:T(8,128)(2,1)} %param.18) | copy-start | bytes 1572868
Sparse Core Ops, SparseCore 0:
  57.0 181.3 all-gather.2
